TPU v7x, 32 devices: a whole 2x2x4 slice. The times are simulated.
32 devices in a mesh: seq: 8 (over z, x), exp: 4 (over y, core).
Axes of the slice: x: 2, y: 2, z: 4, core: 2. Of those that a mesh axis runs over, the one named last changes fastest.
Arguments:
- projected: bfloat16 [4, 1024, 3, 4096], P('exp', 'seq'), may hold values from -8 to 8
- patches: bfloat16 [4, 1024, 4096], P('exp', 'seq'), may hold values from -6 to 6
- norm_gain: float32 [4096], replicated, may hold values from 0.1 to 1.9
- expert_ids: int32 [4, 1024, 2], P('exp', 'seq'), may hold values from 0 to 31, all different within a row; in each aligned block of 128 rows (0 to 127, 128 to 255, ..., all dimensions but the last counted through in order) at most 16 rows name the same one
- gate_levels: int32 [4, 1024, 2], P('exp', 'seq'), may hold values from 1 to 256
- w_gate: bfloat16 [32, 4096, 768], P(('seq', 'exp')), may hold values from -0.09375 to 0.09375
- w_up: bfloat16 [32, 4096, 768], P(('seq', 'exp')), may hold values from -0.09375 to 0.09375
- w_down: bfloat16 [32, 768, 4096], P(('seq', 'exp')), may hold values from -0.21875 to 0.21875
Outputs:
- attended: bfloat16 [4, 1024, 4096], P('exp', 'seq')
- layer_out: bfloat16 [4, 1024, 4096], P('exp', 'seq')
Inputs may be any that keep to these rules, and one draw needn't show every extreme that they name: `expert_ids`: each patch names two different experts. Among the 128 patches of one device (aligned blocks of rows, sequences first), at most 16 name the same expert, and in every draw some expert is named by exactly 16 patches of some device.
All inputs are finite; a program needn't handle non-finite values.
Results may differ from a plain program's by a relative error of at most 0.0068.
Values may be sent and summed in bfloat16 or wider, within the bound.
No kernel may reach another device: no remote copies, remote signals or barrier semaphores. Data moves between devices by JAX's collectives and lax.ppermute only.
A program may use at most 128 MiB of HBM per device.

v0:
```python
import math
import jax
import jax.numpy as jnp
from jax import lax
from jax.sharding import PartitionSpec as P

HEADS = 32


def expert_ffn(arrived, w_gate, w_up, w_down):
    flat_rows = arrived.reshape(-1, arrived.shape[-1])
    gate_part = jnp.dot(flat_rows, w_gate[0], preferred_element_type=jnp.float32)
    up_part = jnp.dot(flat_rows, w_up[0], preferred_element_type=jnp.float32)
    hidden = (jax.nn.silu(gate_part) * up_part).astype(jnp.bfloat16)
    result = jnp.dot(hidden, w_down[0], preferred_element_type=jnp.float32).astype(jnp.bfloat16)
    return result.reshape(arrived.shape[:-1] + (w_down.shape[2],))


def shards(projected, patches, norm_gain, expert_ids, gate_levels, w_gate, w_up, w_down):
    seq_count = lax.axis_size("seq")
    exp_count = lax.axis_size("exp")
    tok_rows = patches.shape[1]
    width = patches.shape[2]
    regrouped = lax.all_to_all(projected, "seq", split_axis=3, concat_axis=1, tiled=True)
    length = regrouped.shape[1]
    local_width = regrouped.shape[3]
    local_heads = HEADS // seq_count
    head_width = local_width // local_heads
    scale = 1.0 / math.sqrt(head_width)
    query_rows = regrouped[0, :, 0].reshape(length, local_heads, head_width)
    key_rows = regrouped[0, :, 1].reshape(length, local_heads, head_width)
    value_rows = regrouped[0, :, 2].reshape(length, local_heads, head_width)
    step_rows = min(512, length)

    def attend(block_index):
        start = block_index * step_rows
        query_part = lax.dynamic_slice_in_dim(query_rows, start, step_rows, 0)
        scores = (
            jnp.einsum("qhd,khd->hqk", query_part, key_rows, preferred_element_type=jnp.float32)
            * scale
        )
        query_pos = start + lax.broadcasted_iota(jnp.int32, (step_rows, length), 0)
        key_pos = lax.broadcasted_iota(jnp.int32, (step_rows, length), 1)
        scores = jnp.where((key_pos <= query_pos)[None], scores, jnp.float32(-1e30))
        highest = jnp.max(scores, axis=-1, keepdims=True)
        weights = jnp.exp(scores - highest)
        probs = (weights / jnp.sum(weights, axis=-1, keepdims=True)).astype(jnp.bfloat16)
        mixed_part = jnp.einsum(
            "hqk,khd->qhd", probs, value_rows, preferred_element_type=jnp.float32
        )
        return mixed_part.astype(jnp.bfloat16).reshape(step_rows, local_width)

    outputs = lax.map(attend, jnp.arange(length // step_rows, dtype=jnp.int32))
    head_major = outputs.reshape(1, length, local_width)
    attended = lax.all_to_all(head_major, "seq", split_axis=1, concat_axis=2, tiled=True)
    stream = (patches.astype(jnp.float32) + attended.astype(jnp.float32)).astype(jnp.bfloat16)
    stream_f = stream.astype(jnp.float32)
    mean_square = jnp.mean(stream_f * stream_f, axis=-1, keepdims=True)
    normed = (stream_f * lax.rsqrt(mean_square + 1e-05) * norm_gain).astype(jnp.bfloat16)
    normed_rows = normed[0]
    expert_count = seq_count * exp_count * w_gate.shape[0]
    capacity = max(2, 4 * tok_rows // expert_count)
    routed = expert_ids[0].reshape(-1)
    onehot = (routed[:, None] == jnp.arange(expert_count, dtype=jnp.int32)[None, :]).astype(
        jnp.int32
    )
    slot = jnp.sum(jnp.cumsum(onehot, axis=0) * onehot, axis=1) - 1
    position = routed * capacity + slot
    selection = jnp.arange(expert_count * capacity, dtype=jnp.int32)[:, None] == position[None, :]
    dispatch_matrix = jnp.any(
        selection.reshape(expert_count * capacity, tok_rows, 2), axis=2
    ).astype(jnp.bfloat16)
    buffer = jnp.dot(dispatch_matrix, normed_rows, preferred_element_type=jnp.float32).astype(
        jnp.bfloat16
    )
    outgoing = buffer.reshape(expert_count, capacity, width)
    processed = expert_ffn(
        lax.all_to_all(outgoing, ("seq", "exp"), split_axis=0, concat_axis=0, tiled=True),
        w_gate,
        w_up,
        w_down,
    )
    returned = lax.all_to_all(processed, ("seq", "exp"), split_axis=0, concat_axis=0, tiled=True)
    flat_back = returned.reshape(expert_count * capacity, width)
    picked = flat_back[position].reshape(tok_rows, 2, width).astype(jnp.float32)
    levels = gate_levels[0].astype(jnp.float32)
    share = levels / jnp.sum(levels, axis=-1, keepdims=True)
    mixture = picked[:, 0, :] * share[:, 0:1] + picked[:, 1, :] * share[:, 1:2]
    layer_out = (stream_f[0] + mixture).astype(jnp.bfloat16)
    return (attended, layer_out[None])


def solution(mesh):
    return jax.shard_map(
        shards,
        mesh=mesh,
        in_specs=(
            P("exp", "seq", None, None),
            P("exp", "seq", None),
            P(),
            P("exp", "seq", None),
            P("exp", "seq", None),
            P(("seq", "exp"), None, None),
            P(("seq", "exp"), None, None),
            P(("seq", "exp"), None, None),
        ),
        out_specs=(P("exp", "seq", None), P("exp", "seq", None)),
        check_vma=False,
    )
```

profile of v0, /device:TPU:0, one launch (start us, length us, event | category | flops | bytes accessed | tf_op | source)
XLA Modules:
  0.0 452.3 jit_solution(14695792651133212737)
XLA Ops:
  0.6 7.2 %copy.54 = bf16[1,128,3,4096]{1,2,0,3:T(4,128)(2,1)} copy(bf16[1,128,3,4096]{3,1,2,0:T(8,128)(2,1)} %param.10) | data formatting | bytes 6291456 | tf_op args[0]
  7.8 7.3 %all-to-all-start = ((bf16[1,128,3,4096]{1,2,0,3:T(4,128)(2,1)}), bf16[1,128,3,4096]{1,2,0,3:T(4,128)(2,1)}, u32[]{:S(2)}, u32[]{:S(2)}) async-start(bf16[1,128,3,4096]{1,2,0,3:T(4,128)(2,1)} %copy.54), calls=%async_computation | async-start | bytes 8388608 | tf_op jit(solution)/shard_map/all_to_all | solution.py:24
  15.1 93.3 %all-to-all-done = bf16[1,128,3,4096]{1,2,0,3:T(4,128)(2,1)} async-done(((bf16[1,128,3,4096]{1,2,0,3:T(4,128)(2,1)}), bf16[1,128,3,4096]{1,2,0,3:T(4,128)(2,1)}, u32[]{:S(2)}, u32[]{:S(2)}) %all-to-all-start) | async-done | bytes 3145760 | tf_op jit(solution)/shard_map/all_to_all | solution.py:24
  108.4 4.8 %copy.81 = bf16[1,128,3,8,512]{1,3,4,2,0:T(8,128)(2,1)S(1)} copy(bf16[1,128,3,8,512]{1,2,4,3,0:T(4,128)(2,1)} %bitcast.3) | data formatting | bytes 6291456 | tf_op jit(solution)/shard_map/all_to_all | solution.py:24
  113.1 3.4 all_to_all.35
  116.5 3.8 fusion.55
  120.3 0.7 copy.57
  120.9 0.0 copy-done.1
  120.9 29.8 %while.10 = (s32[]{:T(128)}, bf16[2,512,512]{2,1,0:T(8,128)(2,1)S(1)}, s32[2]{0:T(128)S(1)}, bf16[1024,4,128]{0,2,1:T(8,128)(2,1)}, bf16[1024,4,128]{2,0,1:T(8,1...) while((s32[]{:T(128)}, ...), condition=%wide.region_3.4_spmd, body=%wide.region_0.3_spmd.sunk | while | flops 1087112704 | bytes 23089332 | solution.py:53
  120.9 0.6 dynamic_slice.22
  122.2 0.4 iota_compare_fusion.5
  122.6 7.5 %fusion.70 = (f32[4,512]{1,0:T(4,128)S(1)}, f32[4,512,1024]{2,1,0:T(8,128)}) fusion(pred[512,1024]{1,0:T(8,128)(4,1)S(1)} %iota_compare_fusion.5, bf16[1024,4,128]{2,0,1:T(8,128)(2,1)S(1)} %get-tuple-element.153, bf16[1024,4,128]{0,2,1:T(8,128)(2,1)} %get-tuple-element.152, s32[]{:T(128)S(6)} %select_n.32), kind=kOutput, calls=%fused_computation.67.clone.1 | convolution fusion | flops 545260544 | bytes 10493956 | tf_op jit(solution)/shard_map/while/body/eval_jaxpr/sub | solution.py:46
  130.1 5.2 %fusion.71 = bf16[4,512,128]{1,2,0:T(8,128)(2,1)S(1)} fusion(bf16[1024,4,128]{0,2,1:T(8,128)(2,1)} %get-tuple-element.154, f32[4,512,1024]{2,1,0:T(8,128)} %get-tuple-element.127, f32[4,512]{1,0:T(4,128)S(1)} %get-tuple-element.128), kind=kOutput, calls=%fused_computation.11.clone.1 | convolution fusion | flops 541327360 | bytes 9969664 | tf_op jit(solution)/shard_map/while/body/eval_jaxpr/hqk,khd->qhd/dot_general | solution.py:48
  135.3 0.2 copy.84
  135.6 0.6 dynamic_slice.22
  136.9 0.4 iota_compare_fusion.5
  137.2 7.5 %fusion.70 = (f32[4,512]{1,0:T(4,128)S(1)}, f32[4,512,1024]{2,1,0:T(8,128)}) fusion(pred[512,1024]{1,0:T(8,128)(4,1)S(1)} %iota_compare_fusion.5, bf16[1024,4,128]{2,0,1:T(8,128)(2,1)S(1)} %get-tuple-element.153, bf16[1024,4,128]{0,2,1:T(8,128)(2,1)} %get-tuple-element.152, s32[]{:T(128)S(6)} %select_n.32), kind=kOutput, calls=%fused_computation.67.clone.1 | convolution fusion | flops 545260544 | bytes 10493956 | tf_op jit(solution)/shard_map/while/body/eval_jaxpr/sub | solution.py:46
  144.8 5.2 %fusion.71 = bf16[4,512,128]{1,2,0:T(8,128)(2,1)S(1)} fusion(bf16[1024,4,128]{0,2,1:T(8,128)(2,1)} %get-tuple-element.154, f32[4,512,1024]{2,1,0:T(8,128)} %get-tuple-element.127, f32[4,512]{1,0:T(4,128)S(1)} %get-tuple-element.128), kind=kOutput, calls=%fused_computation.11.clone.1 | convolution fusion | flops 541327360 | bytes 9969664 | tf_op jit(solution)/shard_map/while/body/eval_jaxpr/hqk,khd->qhd/dot_general | solution.py:48
  150.0 0.2 copy.84
  150.7 1.6 copy.82
  152.4 0.5 broadcast.146
  152.9 7.1 %reduce.4 = bf16[1024,512]{1,0:T(8,128)(2,1)S(1)} reduce(bf16[1024,1,512]{2,1,0:T(2,128)(2,1)S(1)} %bitcast.102, bf16[]{:T(256)} %broadcast.146), dimensions={1}, to_apply=%bitcast.88.reduce_sub_computation | reduce | bytes 2097154
  159.9 0.0 copy-start.2
  159.9 1.6 reshape.239
  161.5 3.6 all-to-all-start.1
  165.2 0.0 copy-done.4
  165.2 0.1 copy.62
  165.3 0.1 eq.40
  165.4 0.1 eq.44
  165.6 0.0 copy-done.2
  165.6 1.3 copy.61
  166.9 0.6 reduce-window.6
  167.5 0.2 slice_reduce_fusion
  167.7 0.1 fusion.46
  167.8 0.1 sub.17
  168.0 0.1 copy.66
  168.0 0.1 fusion.44
  168.1 23.0 %all-to-all-done.1 = bf16[8,2,32768]{2,1,0:T(2,128)(2,1)S(1)} async-done(((bf16[8,2,32768]{2,1,0:T(2,128)(2,1)}), bf16[8,2,32768]{2,1,0:T(2,128)(2,1)S(1)}, u32[]{:S(2)}, u32[]{:S(2)}) %all-to-all-start.1) | async-done | bytes 1048608 | tf_op jit(solution)/shard_map/all_to_all | solution.py:55
  191.1 1.0 reshape.240
  192.2 0.3 copy.74
  192.4 0.0 copy-start.3
  192.5 0.7 copy.60
  193.1 1.8 fusion.31
  195.0 0.0 copy-done.3
  195.0 0.0 slice-start
  195.0 1.7 convolution_convert_fusion
  196.7 0.0 slice-start.1
  196.7 97.1 %all_to_all.46 = bf16[32,16,4096]{2,1,0:T(8,128)(2,1)S(1)} all-to-all(bf16[32,16,4096]{2,1,0:T(8,128)(2,1)S(1)} %bitcast.97), channel_id=1, replica_groups=mesh['seq'=8,'exp'=4] {'seq','exp'}, dimensions={0} | all-to-all | bytes 8388608 | tf_op jit(solution)/shard_map/all_to_all | solution.py:78
  293.8 2.0 copy-done
  295.8 0.0 slice-done
  295.8 0.0 slice-done.1
  295.8 4.6 %fusion.26 = f32[512,768]{1,0:T(8,128)} fusion(bf16[512,4096]{1,0:T(8,128)(2,1)S(1)} %bitcast.105, bf16[1,4096,768]{2,1,0:T(8,128)(2,1)S(1)} %bitcast.114), kind=kOutput, calls=%fused_computation.26 | convolution fusion | flops 3221225472 | bytes 12058624 | tf_op jit(solution)/shard_map/dot_general | solution.py:12
  300.4 17.0 %fusion.28 = bf16[512,4096]{1,0:T(8,128)(2,1)} fusion(bf16[1,768,4096]{2,1,0:T(8,128)(2,1)} %param.17, f32[512,768]{1,0:T(8,128)} %fusion.26, bf16[512,4096]{1,0:T(8,128)(2,1)} %bitcast.106, bf16[1,4096,768]{2,1,0:T(8,128)(2,1)} %param.16), kind=kOutput, calls=%fused_computation.29 | convolution fusion | flops 6446907392 | bytes 22544384 | tf_op jit(solution)/shard_map/dot_general | solution.py:15
  317.4 4.0 all-to-all-start.3
  321.5 0.1 mul.106
  321.7 1.3 copy.69
  323.0 92.7 %all-to-all-done.3 = bf16[32,16,4096]{2,1,0:T(8,128)(2,1)} async-done(((bf16[32,16,4096]{2,1,0:T(8,128)(2,1)}), bf16[32,16,4096]{2,1,0:T(8,128)(2,1)}, u32[]{:S(2)}, u32[]{:S(2)}) %all-to-all-start.3) | async-done | bytes 4194336 | tf_op jit(solution)/shard_map/all_to_all | solution.py:83
  415.7 6.6 %gather_fusion = bf16[256,4096]{1,0:T(8,128)(2,1)S(1)} fusion(bf16[512,4096]{1,0:T(8,128)(2,1)} %bitcast.20, s32[1024]{0:T(1024)S(1)} %pad_clamp_fusion), kind=kCustom, calls=%fused_computation | custom fusion | bytes 4195328 | tf_op jit(solution)/shard_map/gather | solution.py:85
  422.3 4.0 reshape.229
  426.3 9.9 %fusion.54 = (f32[128,1,4096]{2,1,0:T(1,128)}, f32[128,1,4096]{2,1,0:T(1,128)}) fusion(f32[128,2,4096]{2,1,0:T(2,128)} %reshape.229), kind=kLoop, calls=%fused_computation.68 | loop fusion | bytes 8388608 | tf_op jit(solution)/shard_map/slice | solution.py:88
  436.1 5.0 %copy.76 = f32[128,1,4096]{0,2,1:T(8,128)S(1)} copy(f32[128,1,4096]{2,1,0:T(1,128)} %get-tuple-element.82) | data formatting | bytes 4194304
  441.2 5.6 %copy.75 = f32[128,1,4096]{0,2,1:T(8,128)} copy(f32[128,1,4096]{2,1,0:T(1,128)} %get-tuple-element.81) | data formatting | bytes 4194304
  446.8 3.0 fusion.34
  449.8 2.3 copy.70
  (24 shorter events, 0.2 us)
Async XLA Ops:
  7.8 100.6 %all-to-all-start = ((bf16[1,128,3,4096]{1,2,0,3:T(4,128)(2,1)}), bf16[1,128,3,4096]{1,2,0,3:T(4,128)(2,1)}, u32[]{:S(2)}, u32[]{:S(2)}) async-start(bf16[1,128,3,4096]{1,2,0,3:T(4,128)(2,1)} %copy.54), calls=%async_computation | async-start | bytes 8388608 | tf_op jit(solution)/shard_map/all_to_all | solution.py:24
  116.5 4.4 copy-start.1
  152.9 12.3 %copy-start.4 = (s32[1,128,2]{1,2,0:T(2,128)S(1)}, s32[1,128,2]{1,2,0:T(2,128)}, u32[]{:S(2)}) copy-start(s32[1,128,2]{1,2,0:T(2,128)} %param.13) | copy-start | bytes 3076
  159.9 5.6 %copy-start.2 = (bf16[1,128,4096]{2,1,0:T(8,128)(2,1)S(1)}, bf16[1,128,4096]{2,1,0:T(8,128)(2,1)}, u32[]{:S(2)}) copy-start(bf16[1,128,4096]{2,1,0:T(8,128)(2,1)} %param.11) | copy-start | bytes 3145732
  161.5 29.6 %all-to-all-start.1 = ((bf16[8,2,32768]{2,1,0:T(2,128)(2,1)}), bf16[8,2,32768]{2,1,0:T(2,128)(2,1)S(1)}, u32[]{:S(2)}, u32[]{:S(2)}) async-start(bf16[8,2,32768]{2,1,0:T(2,128)(2,1)} %reshape.239), calls=%async_computation.1 | async-start | bytes 2097152 | tf_op jit(solution)/shard_map/all_to_all | solution.py:55
  192.4 2.5 copy-start.3
  195.0 100.8 %slice-start = ((s8[6291456]{0:T(1024)(128)(4,1)}), s8[4194304]{0:T(1024)(128)(4,1)S(1)}, s32[]{:S(2)}) async-start(s8[6291456]{0:T(1024)(128)(4,1)} %bitcast.113), calls=%async_computation.4 | async-start | bytes 8388608
  196.7 99.1 %slice-start.1 = ((s8[6291456]{0:T(1024)(128)(4,1)}), s8[2097152]{0:T(1024)(128)(4,1)S(1)}, s32[]{:S(2)}) async-start(s8[6291456]{0:T(1024)(128)(4,1)} %bitcast.113), calls=%async_computation.5 | async-start | bytes 4194304
  293.8 2.0 copy-start
  317.4 4.2 copy-start.5
  317.4 98.2 %all-to-all-start.3 = ((bf16[32,16,4096]{2,1,0:T(8,128)(2,1)}), bf16[32,16,4096]{2,1,0:T(8,128)(2,1)}, u32[]{:S(2)}, u32[]{:S(2)}) async-start(bf16[32,16,4096]{2,1,0:T(8,128)(2,1)} %bitcast.104), calls=%async_computation.3 | async-start | bytes 8388608 | tf_op jit(solution)/shard_map/all_to_all | solution.py:83
where the time goes:
time: 460 us; the launch traced here: 452 us
  waiting for transfers between devices  209 us (45%)
  blocking collectives  97.1 us (21%)
  local copies, waits for them, and re-layouts  66 us (14%)
  matrix products  48.8 us (11%)
  starting transfers between devices  14.9 us (3%)
  other arithmetic  13.5 us (3%)
    all_to_all x1, blocking collectives, shards(): lax.all_to_all(outgoing, ('seq', 'exp'), split_axis=0, concat_axis=0, til...  97.1 us
    all_to_all x1, waiting for transfers between devices, shards(): lax.all_to_all(projected, 'seq', split_axis=3, concat_axis=1, tiled=True)  93.3 us
    all_to_all x1, waiting for transfers between devices, shards(): lax.all_to_all(processed, ('seq', 'exp'), split_axis=0, concat_axis=0, ti...  92.7 us
    unnamed x27, local copies, waits for them, and re-layouts  28.3 us
    all_to_all x1, waiting for transfers between devices, shards(): lax.all_to_all(head_major, 'seq', split_axis=1, concat_axis=2, tiled=True)  23 us
    dot_general x1, matrix products, expert_ffn(): jnp.dot(hidden, w_down[0], preferred_element_type=jnp.float32)  17 us
    sub x2, matrix products, attend(): weights = jnp.exp(scores - highest)  15.1 us
    dot_general x2, matrix products, attend(): jnp.einsum('hqk,khd->qhd', probs, value_rows, preferred_element_type=jnp....  10.4 us
  transfers between devices with their start and end apart: 3, of which 3 were waited for; matrix products, arithmetic and copies ran while one was open for 1% of the time, Pallas kernels for 0%

commit v1 on v0

--- a/solution.py
+++ b/solution.py
@@ -5,6 +5,22 @@
 from jax.sharding import PartitionSpec as P
 
 HEADS = 32
+
+
+def pairwise_exchange(value, axis, split, join):
+    ways, here = (lax.axis_size(axis), lax.axis_index(axis))
+    width = value.shape[split] // ways
+    shape = list(value.shape)
+    shape[split] = width
+    height = shape[join]
+    shape[join] = height * ways
+    full = jnp.zeros(shape, value.dtype)
+    for mask in range(ways):
+        part = lax.dynamic_slice_in_dim(value, (here ^ mask) * width, width, axis=split)
+        if mask:
+            part = lax.ppermute(part, axis, [(d, d ^ mask) for d in range(ways)])
+        full = lax.dynamic_update_slice_in_dim(full, part, (here ^ mask) * height, axis=join)
+    return full
 
 
 def expert_ffn(arrived, w_gate, w_up, w_down):
@@ -52,7 +68,7 @@
 
     outputs = lax.map(attend, jnp.arange(length // step_rows, dtype=jnp.int32))
     head_major = outputs.reshape(1, length, local_width)
-    attended = lax.all_to_all(head_major, "seq", split_axis=1, concat_axis=2, tiled=True)
+    attended = pairwise_exchange(head_major, "seq", 1, 2)
     stream = (patches.astype(jnp.float32) + attended.astype(jnp.float32)).astype(jnp.bfloat16)
     stream_f = stream.astype(jnp.float32)
     mean_square = jnp.mean(stream_f * stream_f, axis=-1, keepdims=True)

time: 460 us -> 428 us (0.930); the launches traced: 452 us -> 428 us
  local copies, waits for them, and re-layouts: 66 us -> 46.5 us
  waiting for transfers between devices: 209 us -> 201 us
  starting transfers between devices: 14.9 us -> 22 us
  other arithmetic: 13.5 us -> 7.22 us
    all_to_all x1 -> x0, waiting for transfers between devices: 23 us -> none  [shards(): lax.all_to_all(head_major, 'seq', split_axis=1, concat_axis=2, tiled=True)]
    unnamed x27 -> x24, local copies, waits for them, and re-layouts: 28.3 us -> 9.33 us
    ppermute x0 -> x7, waiting for transfers between devices: none -> 15.3 us  [pairwise_exchange(): part = lax.ppermute(part, axis, [(d, d ^ mask) for d in range(ways)])]
    ppermute x0 -> x7, starting transfers between devices: none -> 10.6 us  [pairwise_exchange(): part = lax.ppermute(part, axis, [(d, d ^ mask) for d in range(ways)])]
    unnamed x2 -> x1, other arithmetic: 7.06 us -> 0.01 us
  transfers between devices with their start and end apart: 3 -> 9, of which waited for: 3 -> 5; matrix products, arithmetic and copies ran while one was open for 1% -> 0% of each run, Pallas kernels for 0% -> 0%
where the time goes in v1:
time: 428 us
  waiting for transfers between devices  201 us (47%)
  blocking collectives  99.9 us (23%)
  matrix products  48.6 us (11%)
  local copies, waits for them, and re-layouts  46.5 us (11%)
  starting transfers between devices  22 us (5%)
  other arithmetic  7.22 us (2%)
    all_to_all x1, blocking collectives, shards(): lax.all_to_all(outgoing, ('seq', 'exp'), split_axis=0, concat_axis=0, til...  99.9 us
    all_to_all x1, waiting for transfers between devices, shards(): lax.all_to_all(processed, ('seq', 'exp'), split_axis=0, concat_axis=0, ti...  93.8 us
    all_to_all x1, waiting for transfers between devices, shards(): lax.all_to_all(projected, 'seq', split_axis=3, concat_axis=1, tiled=True)  91.7 us
    dot_general x1, matrix products, expert_ffn(): jnp.dot(hidden, w_down[0], preferred_element_type=jnp.float32)  17 us
    ppermute x7, waiting for transfers between devices, pairwise_exchange(): part = lax.ppermute(part, axis, [(d, d ^ mask) for d in range(ways)])  15.3 us
    sub x2, matrix products, attend(): weights = jnp.exp(scores - highest)  15.2 us
    ppermute x7, starting transfers between devices, pairwise_exchange(): part = lax.ppermute(part, axis, [(d, d ^ mask) for d in range(ways)])  10.6 us
    dot_general x2, matrix products, attend(): jnp.einsum('hqk,khd->qhd', probs, value_rows, preferred_element_type=jnp....  10.4 us
  transfers between devices with their start and end apart: 9, of which 5 were waited for; matrix products, arithmetic and copies ran while one was open for 0% of the time, Pallas kernels for 0%

profile of v1, /device:TPU:0, one launch (start us, length us, event | category | flops | bytes accessed | tf_op | source)
XLA Modules:
  0.0 427.8 jit_solution(7855601794367231271)
XLA Ops:
  0.6 7.2 %copy.36 = bf16[1,128,3,4096]{1,2,0,3:T(4,128)(2,1)} copy(bf16[1,128,3,4096]{3,1,2,0:T(8,128)(2,1)} %param.10) | data formatting | bytes 6291456 | tf_op args[0]
  7.8 7.4 %all-to-all-start = ((bf16[1,128,3,4096]{1,2,0,3:T(4,128)(2,1)}), bf16[1,128,3,4096]{1,2,0,3:T(4,128)(2,1)}, u32[]{:S(2)}, u32[]{:S(2)}) async-start(bf16[1,128,3,4096]{1,2,0,3:T(4,128)(2,1)} %copy.36), calls=%async_computation | async-start | bytes 8388608 | tf_op jit(solution)/shard_map/all_to_all | solution.py:40
  15.3 0.0 copy-done.7
  15.3 0.1 copy.41
  15.4 0.1 eq.40
  15.5 0.1 eq.44
  15.7 0.6 reduce-window.6
  16.3 0.2 slice_reduce_fusion
  16.5 0.1 fusion.48
  16.6 0.0 copy-start.5
  16.6 0.1 sub.17
  16.8 91.7 %all-to-all-done = bf16[1,128,3,4096]{1,2,0,3:T(4,128)(2,1)} async-done(((bf16[1,128,3,4096]{1,2,0,3:T(4,128)(2,1)}), bf16[1,128,3,4096]{1,2,0,3:T(4,128)(2,1)}, u32[]{:S(2)}, u32[]{:S(2)}) %all-to-all-start) | async-done | bytes 3145760 | tf_op jit(solution)/shard_map/all_to_all | solution.py:40
  108.5 0.0 copy-done.5
  108.5 4.8 %copy.68 = bf16[1,128,3,8,512]{1,3,4,2,0:T(8,128)(2,1)S(1)} copy(bf16[1,128,3,8,512]{1,2,4,3,0:T(4,128)(2,1)} %bitcast.3) | data formatting | bytes 6291456 | tf_op jit(solution)/shard_map/all_to_all | solution.py:40
  113.3 3.3 all_to_all.22
  116.6 3.7 fusion.57
  120.3 0.7 copy.39
  121.0 0.0 copy-done.3
  121.0 29.7 %while.10 = (s32[]{:T(128)}, bf16[2,512,512]{2,1,0:T(8,128)(2,1)S(1)}, s32[2]{0:T(128)S(1)}, bf16[1024,4,128]{0,2,1:T(8,128)(2,1)}, bf16[1024,4,128]{2,0,1:T(8,1...) while((s32[]{:T(128)}, ...), condition=%wide.region_3.4_spmd, body=%wide.region_0.3_spmd.sunk | while | flops 1087112704 | bytes 23089332 | solution.py:69
  121.0 0.6 dynamic_slice.62
  122.2 0.4 iota_compare_fusion.5
  122.6 7.6 %fusion.72 = (f32[4,512]{1,0:T(4,128)S(1)}, f32[4,512,1024]{2,1,0:T(8,128)}) fusion(pred[512,1024]{1,0:T(8,128)(4,1)S(1)} %iota_compare_fusion.5, bf16[1024,4,128]{2,0,1:T(8,128)(2,1)S(1)} %get-tuple-element.147, bf16[1024,4,128]{0,2,1:T(8,128)(2,1)} %get-tuple-element.146, s32[]{:T(128)S(6)} %select_n.96), kind=kOutput, calls=%fused_computation.84.clone.1 | convolution fusion | flops 545260544 | bytes 10493956 | tf_op jit(solution)/shard_map/while/body/eval_jaxpr/sub | solution.py:62
  130.2 5.2 %fusion.73 = bf16[4,512,128]{1,2,0:T(8,128)(2,1)S(1)} fusion(bf16[1024,4,128]{0,2,1:T(8,128)(2,1)} %get-tuple-element.148, f32[4,512,1024]{2,1,0:T(8,128)} %get-tuple-element.121, f32[4,512]{1,0:T(4,128)S(1)} %get-tuple-element.122), kind=kOutput, calls=%fused_computation.11.clone.1 | convolution fusion | flops 541327360 | bytes 9969664 | tf_op jit(solution)/shard_map/while/body/eval_jaxpr/hqk,khd->qhd/dot_general | solution.py:64
  135.4 0.2 copy.70
  135.7 0.6 dynamic_slice.62
  137.0 0.4 iota_compare_fusion.5
  137.4 7.6 %fusion.72 = (f32[4,512]{1,0:T(4,128)S(1)}, f32[4,512,1024]{2,1,0:T(8,128)}) fusion(pred[512,1024]{1,0:T(8,128)(4,1)S(1)} %iota_compare_fusion.5, bf16[1024,4,128]{2,0,1:T(8,128)(2,1)S(1)} %get-tuple-element.147, bf16[1024,4,128]{0,2,1:T(8,128)(2,1)} %get-tuple-element.146, s32[]{:T(128)S(6)} %select_n.96), kind=kOutput, calls=%fused_computation.84.clone.1 | convolution fusion | flops 545260544 | bytes 10493956 | tf_op jit(solution)/shard_map/while/body/eval_jaxpr/sub | solution.py:62
  145.0 5.2 %fusion.73 = bf16[4,512,128]{1,2,0:T(8,128)(2,1)S(1)} fusion(bf16[1024,4,128]{0,2,1:T(8,128)(2,1)} %get-tuple-element.148, f32[4,512,1024]{2,1,0:T(8,128)} %get-tuple-element.121, f32[4,512]{1,0:T(4,128)S(1)} %get-tuple-element.122), kind=kOutput, calls=%fused_computation.11.clone.1 | convolution fusion | flops 541327360 | bytes 9969664 | tf_op jit(solution)/shard_map/while/body/eval_jaxpr/hqk,khd->qhd/dot_general | solution.py:64
  150.2 0.2 copy.70
  150.7 0.0 copy-start.1
  150.7 0.1 broadcast_in_dim.23
  150.8 0.0 copy-start.4
  150.8 0.9 constant_dynamic-slice_fusion
  151.6 1.5 collective-permute-start
  153.1 0.1 copy.45
  153.2 0.0 collective-permute-start.1
  153.2 0.1 fusion.46
  153.3 2.1 collective-permute-start.2
  155.4 0.8 collective-permute-start.3
  156.2 3.0 collective-permute-start.4
  159.2 0.0 collective-permute-done
  159.2 1.5 collective-permute-start.5
  160.7 1.7 collective-permute-done.1
  162.4 1.7 collective-permute-start.6
  164.2 0.0 collective-permute-done.2
  164.2 9.8 %collective-permute-done.3 = bf16[1,128,512]{2,1,0:T(8,128)(2,1)S(1)} collective-permute-done((bf16[1,128,512]{2,1,0:T(8,128)(2,1)}, bf16[1,128,512]{2,1,0:T(8,128)(2,1)S(1)}, u32[]{:S(2)}, u32[]{:S(2)}) %collective-permute-start.3) | collective-permute-done | bytes 131104 | tf_op jit(solution)/shard_map/ppermute | solution.py:21
  174.1 3.7 collective-permute-done.4
  177.8 0.0 collective-permute-done.5
  177.8 0.0 collective-permute-done.6
  177.9 0.0 copy-start
  177.9 0.4 fusion.31
  178.4 0.0 slice-start.1
  178.4 1.3 convolution_convert_fusion
  179.7 99.9 %all_to_all.28 = bf16[32,16,4096]{2,1,0:T(8,128)(2,1)S(1)} all-to-all(bf16[32,16,4096]{2,1,0:T(8,128)(2,1)S(1)} %bitcast.91), channel_id=1, replica_groups=mesh['seq'=8,'exp'=4] {'seq','exp'}, dimensions={0} | all-to-all | bytes 8388608 | tf_op jit(solution)/shard_map/all_to_all | solution.py:94
  279.6 2.0 copy-done.2
  281.6 4.6 %fusion.26 = f32[512,768]{1,0:T(8,128)} fusion(bf16[512,4096]{1,0:T(8,128)(2,1)S(1)} %bitcast.95, bf16[1,4096,768]{2,1,0:T(8,128)(2,1)S(1)} %bitcast.104), kind=kOutput, calls=%fused_computation.26 | convolution fusion | flops 3221225472 | bytes 12058624 | tf_op jit(solution)/shard_map/dot_general | solution.py:28
  286.2 17.0 %fusion.28 = bf16[512,4096]{1,0:T(8,128)(2,1)} fusion(bf16[1,768,4096]{2,1,0:T(8,128)(2,1)} %param.17, f32[512,768]{1,0:T(8,128)} %fusion.26, bf16[512,4096]{1,0:T(8,128)(2,1)} %bitcast.96, bf16[1,4096,768]{2,1,0:T(8,128)(2,1)} %param.16), kind=kOutput, calls=%fused_computation.29 | convolution fusion | flops 6446907392 | bytes 22544384 | tf_op jit(solution)/shard_map/dot_general | solution.py:31
  303.2 4.0 all-to-all-start.2
  307.2 0.1 mul.170
  307.5 93.8 %all-to-all-done.2 = bf16[32,16,4096]{2,1,0:T(8,128)(2,1)} async-done(((bf16[32,16,4096]{2,1,0:T(8,128)(2,1)}), bf16[32,16,4096]{2,1,0:T(8,128)(2,1)}, u32[]{:S(2)}, u32[]{:S(2)}) %all-to-all-start.2) | async-done | bytes 4194336 | tf_op jit(solution)/shard_map/all_to_all | solution.py:99
  401.3 7.9 %gather_fusion = bf16[256,4096]{1,0:T(8,128)(2,1)} fusion(bf16[512,4096]{1,0:T(8,128)(2,1)} %bitcast.18, s32[1024]{0:T(1024)S(1)} %pad_clamp_fusion), kind=kCustom, calls=%fused_computation | custom fusion | bytes 4195328 | tf_op jit(solution)/shard_map/gather | solution.py:101
  409.2 5.5 %reshape.217 = f32[128,2,4096]{2,1,0:T(2,128)} reshape(bf16[256,4096]{1,0:T(8,128)(2,1)} %gather_fusion) | data formatting | bytes 6291456 | tf_op jit(solution)/shard_map/convert_element_type | solution.py:101
  414.7 7.9 %fusion.56 = (f32[128,1,4096]{2,1,0:T(1,128)S(1)}, f32[128,1,4096]{2,1,0:T(1,128)S(1)}) fusion(f32[128,2,4096]{2,1,0:T(2,128)} %reshape.217), kind=kLoop, calls=%fused_computation.85 | loop fusion | bytes 8388608 | tf_op jit(solution)/shard_map/slice | solution.py:104
  422.6 5.2 %fusion.34 = bf16[1,128,4096]{2,1,0:T(8,128)(2,1)} fusion(f32[128,1,4096]{2,1,0:T(1,128)S(1)} %get-tuple-element.68, f32[128,1,4096]{2,1,0:T(1,128)S(1)} %get-tuple-element.67, f32[128]{0:T(128)S(1)} %get-tuple-element.81, f32[128]{0:T(128)S(1)} %get-tuple-element.80, bf16[1,128,4096]{2,1,0:T(8,128)(2,1)S(1)} %constant_dynamic-update-slice_fusion.1, ...), kind=kLoop, calls=%fused_computation.37 | loop fusion | flops 5242880 | bytes 7341056 | tf_op jit(solution)/shard_map/convert_element_type | solution.py:105
  (39 shorter events, 0.3 us)
Async XLA Ops:
  7.8 7.4 %copy-start.7 = (s32[1,128,2]{1,2,0:T(2,128)S(1)}, s32[1,128,2]{1,2,0:T(2,128)}, u32[]{:S(2)}) copy-start(s32[1,128,2]{1,2,0:T(2,128)} %param.13) | copy-start | bytes 3076
  7.8 100.7 %all-to-all-start = ((bf16[1,128,3,4096]{1,2,0,3:T(4,128)(2,1)}), bf16[1,128,3,4096]{1,2,0,3:T(4,128)(2,1)}, u32[]{:S(2)}, u32[]{:S(2)}) async-start(bf16[1,128,3,4096]{1,2,0,3:T(4,128)(2,1)} %copy.36), calls=%async_computation | async-start | bytes 8388608 | tf_op jit(solution)/shard_map/all_to_all | solution.py:40
  16.6 91.9 %copy-start.5 = (s32[256]{0:T(256)}, s32[256]{0:T(256)S(1)}, u32[]{:S(2)}) copy-start(s32[256]{0:T(256)S(1)} %broadcast_add_fusion) | copy-start | bytes 3076
  116.6 4.3 %copy-start.3 = (bf16[2,512,512]{2,1,0:T(8,128)(2,1)S(1)}, bf16[2,512,512]{2,1,0:T(8,128)(2,1)}, u32[]{:S(2)}) copy-start(bf16[2,512,512]{2,1,0:T(8,128)(2,1)} %custom-call.2) | copy-start | bytes 3145732
  150.7 27.2 %copy-start.1 = (bf16[1,128,4096]{2,1,0:T(8,128)(2,1)S(1)}, bf16[1,128,4096]{2,1,0:T(8,128)(2,1)}, u32[]{:S(2)}) copy-start(bf16[1,128,4096]{2,1,0:T(8,128)(2,1)} %param.11) | copy-start | bytes 3145732
  150.8 27.6 %copy-start.4 = (f32[4096]{0:T(1024)S(1)}, f32[4096]{0:T(1024)}, u32[]{:S(2)}) copy-start(f32[4096]{0:T(1024)} %param.12) | copy-start | bytes 49156
  151.6 7.6 %collective-permute-start = (bf16[1,128,512]{2,1,0:T(8,128)(2,1)}, bf16[1,128,512]{2,1,0:T(8,128)(2,1)S(1)}, u32[]{:S(2)}, u32[]{:S(2)}) collective-permute-start(bf16[1,128,512]{2,1,0:T(8,128)(2,1)} %get-tuple-element.78), channel_id=1, source_target_pairs={{0,4},{4,0},{8,12},{12,8},{16,20},{20,16},{24,28},{28,24},{1,5},{5... | collective-permute-start | bytes 393224 | tf_op jit(solution)/shard_map/ppermute | solution.py:21
  153.2 9.3 %collective-permute-start.1 = (bf16[1,128,512]{2,1,0:T(8,128)(2,1)}, bf16[1,128,512]{2,1,0:T(8,128)(2,1)S(1)}, u32[]{:S(2)}, u32[]{:S(2)}) collective-permute-start(bf16[1,128,512]{2,1,0:T(8,128)(2,1)} %get-tuple-element.77), channel_id=1, source_target_pairs={{0,8},{4,12},{8,0},{12,4},{16,24},{20,28},{24,16},{28,20},{1,9},{5... | collective-permute-start | bytes 393224 | tf_op jit(solution)/shard_map/ppermute | solution.py:21
  153.3 10.9 %collective-permute-start.2 = (bf16[1,128,512]{2,1,0:T(8,128)(2,1)}, bf16[1,128,512]{2,1,0:T(8,128)(2,1)S(1)}, u32[]{:S(2)}, u32[]{:S(2)}) collective-permute-start(bf16[1,128,512]{2,1,0:T(8,128)(2,1)} %get-tuple-element.76), channel_id=1, source_target_pairs={{0,12},{4,8},{8,4},{12,0},{16,28},{20,24},{24,20},{28,16},{1,13},{... | collective-permute-start | bytes 393224 | tf_op jit(solution)/shard_map/ppermute | solution.py:21
  155.4 18.6 %collective-permute-start.3 = (bf16[1,128,512]{2,1,0:T(8,128)(2,1)}, bf16[1,128,512]{2,1,0:T(8,128)(2,1)S(1)}, u32[]{:S(2)}, u32[]{:S(2)}) collective-permute-start(bf16[1,128,512]{2,1,0:T(8,128)(2,1)} %get-tuple-element.75), channel_id=1, source_target_pairs={{0,16},{4,20},{8,24},{12,28},{16,0},{20,4},{24,8},{28,12},{1,17},{... | collective-permute-start | bytes 393224 | tf_op jit(solution)/shard_map/ppermute | solution.py:21
  156.2 21.6 %collective-permute-start.4 = (bf16[1,128,512]{2,1,0:T(8,128)(2,1)}, bf16[1,128,512]{2,1,0:T(8,128)(2,1)S(1)}, u32[]{:S(2)}, u32[]{:S(2)}) collective-permute-start(bf16[1,128,512]{2,1,0:T(8,128)(2,1)} %get-tuple-element.74), channel_id=1, source_target_pairs={{0,20},{4,16},{8,28},{12,24},{16,4},{20,0},{24,12},{28,8},{1,21},{... | collective-permute-start | bytes 393224 | tf_op jit(solution)/shard_map/ppermute | solution.py:21
  159.2 18.6 %collective-permute-start.5 = (bf16[1,128,512]{2,1,0:T(8,128)(2,1)S(1)}, bf16[1,128,512]{2,1,0:T(8,128)(2,1)S(1)}, u32[]{:S(2)}, u32[]{:S(2)}) collective-permute-start(bf16[1,128,512]{2,1,0:T(8,128)(2,1)S(1)} %get-tuple-element.73), channel_id=1, source_target_pairs={{0,24},{4,28},{8,16},{12,20},{16,8},{20,12},{24,0},{28,4},{1,25},{... | collective-permute-start | bytes 393224 | tf_op jit(solution)/shard_map/ppermute | solution.py:21
  162.4 15.4 %collective-permute-start.6 = (bf16[1,128,512]{2,1,0:T(8,128)(2,1)S(1)}, bf16[1,128,512]{2,1,0:T(8,128)(2,1)S(1)}, u32[]{:S(2)}, u32[]{:S(2)}) collective-permute-start(bf16[1,128,512]{2,1,0:T(8,128)(2,1)S(1)} %get-tuple-element.72), channel_id=1, source_target_pairs={{0,28},{4,24},{8,20},{12,16},{16,12},{20,8},{24,4},{28,0},{1,29},{... | collective-permute-start | bytes 393224 | tf_op jit(solution)/shard_map/ppermute | solution.py:21
  174.0 107.5 %slice-start = ((s8[6291456]{0:T(1024)(128)(4,1)}), s8[4194304]{0:T(1024)(128)(4,1)S(1)}, s32[]{:S(2)}) async-start(s8[6291456]{0:T(1024)(128)(4,1)} %bitcast.103), calls=%async_computation.3 | async-start | bytes 8388608
  177.9 244.7 %copy-start = (bf16[1,128,4096]{2,1,0:T(8,128)(2,1)}, bf16[1,128,4096]{2,1,0:T(8,128)(2,1)S(1)}, u32[]{:S(2)}) copy-start(bf16[1,128,4096]{2,1,0:T(8,128)(2,1)S(1)} %constant_dynamic-update-slice_fusion.1) | copy-start | bytes 3145732
  178.4 103.2 %slice-start.1 = ((s8[6291456]{0:T(1024)(128)(4,1)}), s8[2097152]{0:T(1024)(128)(4,1)S(1)}, s32[]{:S(2)}) async-start(s8[6291456]{0:T(1024)(128)(4,1)} %bitcast.103), calls=%async_computation.4 | async-start | bytes 4194304
  279.6 2.0 copy-start.2
  303.2 4.2 copy-start.8
  303.2 4.2 copy-start.6
  303.2 98.1 %all-to-all-start.2 = ((bf16[32,16,4096]{2,1,0:T(8,128)(2,1)}), bf16[32,16,4096]{2,1,0:T(8,128)(2,1)}, u32[]{:S(2)}, u32[]{:S(2)}) async-start(bf16[32,16,4096]{2,1,0:T(8,128)(2,1)} %bitcast.94), calls=%async_computation.2 | async-start | bytes 8388608 | tf_op jit(solution)/shard_map/all_to_all | solution.py:99
